TPU v7x, 128 devices: a whole 4x4x4 slice. The times are simulated.
128 devices in a mesh: row: 8 (over z_lo, x), col: 16 (over y, z_hi, core).
Axes of the slice: x: 4, y: 4, z: 4 (z_hi: 2, z_lo: 2; z = z_hi * 2 + z_lo), core: 2. Of those that a mesh axis runs over, the one named last changes fastest.
Arguments:
- positions: float32 [3, 16384, 128], P(None, ('row', 'col')), may hold values from -6 to 6
- block_links: int32 [2, 16384], replicated, may hold values from 0 to 16383, as said below
- panel_points: int32 [8, 256], replicated, may hold values from 0 to 2097151
Outputs:
- smoothed: float32 [3, 32768, 128], P(None, ('row', 'col'))
- velocity: float32 [8, 3, 256], P('row', None, 'col')
Inputs may be any that keep to these rules, and one draw needn't show every extreme that they name: block_links[0, b] is an owner device, numbered in the order of row+col; block_links[1] is a permutation of the 16384 blocks whose cycles are the loops, and all blocks of one loop have one owner. The 128 blocks of one device, b // 128, include at most 2 of any one owner, and in every draw one owner has exactly 2 blocks on every device.
All inputs are finite; a program needn't handle non-finite values.
Results may differ from a plain program's by a relative error of at most 0.0003.
Values sent between devices are 32-bit elements; how exact they have to be, the bound alone decides.
A program may use at most 128 MiB of HBM per device.

v0:
```python
import math
import jax
import jax.numpy as jnp
from jax import lax
from jax.sharding import PartitionSpec as P

SWEEPS = 2
SMOOTH_RATE = 0.25
CORE_SQUARED = 0.01


def cross_three(left_vec, right_vec):
    return jnp.stack(
        [
            left_vec[1] * right_vec[2] - left_vec[2] * right_vec[1],
            left_vec[2] * right_vec[0] - left_vec[0] * right_vec[2],
            left_vec[0] * right_vec[1] - left_vec[1] * right_vec[0],
        ]
    )


def neighbours(points, next_slot, prev_slot):
    ahead = jnp.concatenate([points[:, :, 1:], points[:, next_slot, :1]], axis=2)
    behind = jnp.concatenate([points[:, prev_slot, -1:], points[:, :, :-1]], axis=2)
    return (behind, ahead)


def smooth_loops(points, next_slot, prev_slot):
    for sweep_no in range(SWEEPS):
        behind, ahead = neighbours(points, next_slot, prev_slot)
        points = points + SMOOTH_RATE * (behind - 2.0 * points + ahead)
    return points


def panel_sums(targets, sources):
    centres = sources[:3]
    segments = sources[3:]
    inner = lax.dot_general(
        targets, centres, (((0,), (0,)), ((), ())), precision=lax.Precision.HIGHEST
    )
    squared = (
        jnp.sum(targets * targets, 0)[:, None]
        + jnp.sum(centres * centres, 0)[None, :]
        - 2.0 * inner
        + CORE_SQUARED
    )
    weights = 1.0 / (squared * jnp.sqrt(squared))
    features = jnp.concatenate([segments, cross_three(segments, centres)], 0)
    return lax.dot_general(
        weights, features, (((1,), (1,)), ((), ())), precision=lax.Precision.HIGHEST
    )


def tiled_sums(targets, piece, running, largest):
    blocks = piece.shape[1]
    block_len = piece.shape[2]
    group = max(
        [
            size_try
            for size_try in (1, 2, 4, 8, 16, 32, 64, 128)
            if blocks % size_try == 0 and size_try <= largest
        ]
    )

    def one_tile(turn, accum):
        tile = lax.dynamic_slice_in_dim(piece, turn * group, group, 1).reshape(6, group * block_len)
        return accum + panel_sums(targets, tile)

    return lax.fori_loop(0, blocks // group, one_tile, running)


def shards(positions, block_links, panel_points):
    devices = lax.axis_size(("row", "col"))
    my_index = lax.axis_index(("row", "col"))
    slots = positions.shape[1]
    block_len = positions.shape[2]
    capacity = 2 * slots // devices
    held_slots = devices * capacity
    owners = block_links[0]
    follows = block_links[1]
    blocks_all = owners.shape[0]
    counter = jnp.arange(blocks_all, dtype=jnp.int32)
    precedes = jnp.zeros_like(follows).at[follows].set(counter)
    owner_grid = owners.reshape(devices, slots)
    same_owner = owner_grid[:, :, None] == owner_grid[:, None, :]
    earlier = jnp.arange(slots)[None, :] < jnp.arange(slots)[:, None]
    ranks = jnp.sum(jnp.logical_and(same_owner, earlier[None]), axis=2).reshape(blocks_all)
    places = counter // slots * capacity + ranks
    my_owner = lax.dynamic_slice_in_dim(owners, my_index * slots, slots)
    my_rank = lax.dynamic_slice_in_dim(ranks, my_index * slots, slots)
    outgoing_slot = my_owner * capacity + my_rank
    outgoing = (
        jnp.zeros((3, held_slots, block_len), jnp.float32).at[:, outgoing_slot, :].set(positions)
    )
    arrived = lax.all_to_all(outgoing, ("row", "col"), split_axis=1, concat_axis=1, tiled=True)
    is_owned = owners == my_index
    held_ids = (
        jnp.full((held_slots,), blocks_all, jnp.int32)
        .at[jnp.where(is_owned, places, held_slots)]
        .set(counter, mode="drop")
    )
    live = held_ids < blocks_all
    safe_ids = jnp.minimum(held_ids, blocks_all - 1)
    slot_index = jnp.arange(held_slots, dtype=jnp.int32)
    next_slot = jnp.where(live, places[follows[safe_ids]], slot_index)
    prev_slot = jnp.where(live, places[precedes[safe_ids]], slot_index)
    smoothed = smooth_loops(arrived, next_slot, prev_slot)
    behind, ahead = neighbours(smoothed, next_slot, prev_slot)
    segments = ahead - smoothed
    centres = 0.5 * (ahead + smoothed)
    sources = jnp.concatenate([centres, segments], 0)
    wanted = panel_points.reshape(-1)
    wanted_block = wanted // block_len
    wanted_point = wanted % block_len
    wanted_mine = owners[wanted_block] == my_index
    picked = smoothed[:, places[wanted_block], wanted_point]
    local_targets = jnp.where(wanted_mine[None, :], picked, 0.0)
    all_targets = lax.psum(local_targets, ("row", "col"))
    panel = panel_points.shape[1]
    col_count = lax.axis_size("col")
    share = panel // col_count
    scale = 1.0 / (math.pi * math.sqrt(blocks_all * block_len))
    targets = lax.dynamic_slice_in_dim(all_targets, lax.axis_index("row") * panel, panel, 1)
    zero_sums = jnp.zeros((panel, 6), jnp.float32)
    sums = tiled_sums(targets, lax.all_gather(sources, "row", axis=1, tiled=True), zero_sums, 128)
    partial_velocity = scale * (cross_three(sums[:, :3].T, targets) - sums[:, 3:].T)
    summed = lax.psum(partial_velocity, "col")
    velocity_part = lax.dynamic_slice_in_dim(summed, lax.axis_index("col") * share, share, 1)
    return (smoothed, velocity_part[None])


def solution(mesh):
    placed = (P(None, ("row", "col"), None), P(), P())
    return jax.shard_map(
        shards,
        mesh=mesh,
        in_specs=placed,
        out_specs=(P(None, ("row", "col"), None), P("row", None, "col")),
        check_vma=False,
    )
```

profile of v0, /device:TPU:0, one launch (start us, length us, event | category | flops | bytes accessed | tf_op | source)
XLA Modules:
  0.0 976.3 jit_solution(4487103491891929501)
XLA Ops:
  15.4 12.5 %scatter_fusion = f32[3,256,128]{2,0,1:T(4,128)} fusion(f32[3,256,128]{2,0,1:T(4,128)} %broadcast_in_dim.36, s32[128]{0:T(128)S(1)} %compare_select_fusion.13, f32[128,3,128]{2,1,0:T(4,128)S(1)} %copy.77), kind=kCustom, calls=%fused_computation.12 | custom fusion | bytes 590336 | tf_op jit(solution)/shard_map/scatter | solution.py:93
  27.9 11.2 %all-to-all-start = ((f32[3,256,128]{2,0,1:T(4,128)}), f32[3,256,128]{2,0,1:T(4,128)S(1)}, u32[]{:S(2)}, u32[]{:S(2)}) async-start(f32[3,256,128]{2,0,1:T(4,128)} %scatter_fusion), calls=%async_computation | async-start | bytes 1048576 | tf_op jit(solution)/shard_map/all_to_all | solution.py:95
  40.4 60.3 %scatter_custom_fusion.1 = s32[256]{0:T(256)S(1)} fusion(s32[16384]{0:T(1024)S(1)} %bitcast.119, s32[16384]{0:T(1024)S(1)} %iota.31, s32[]{:T(128)} %constant.150.clone.1), kind=kCustom, calls=%fused_computation.120 | custom fusion | bytes 1028 | tf_op jit(solution)/shard_map/scatter | solution.py:100
  100.8 60.5 %scatter_custom_fusion.2 = s32[16384]{0:T(1024)S(1)} fusion(s32[16384]{0:T(1024)S(1)} %bitcast.118, s32[16384]{0:T(1024)S(1)} %iota.33, s32[]{:T(128)} %constant.144.clone.1), kind=kCustom, calls=%fused_computation.79 | custom fusion | bytes 65540 | tf_op jit(solution)/shard_map/scatter | solution.py:83
  217.9 11.8 %gather_fusion.9 = s32[2048]{0:T(1024)S(1)} fusion(s32[16384]{0:T(1024)S(1)} %fusion.28, s32[2048]{0:T(1024)S(1)} %broadcast_clamp_fusion), kind=kCustom, calls=%fused_computation.9 | custom fusion | bytes 24576 | tf_op jit(solution)/shard_map/gather | solution.py:116
  229.7 11.8 %gather_fusion.8 = s32[2048]{0:T(1024)S(1)} fusion(s32[16384]{0:T(1024)S(1)} %bitcast.99, s32[2048]{0:T(1024)S(1)} %broadcast_clamp_fusion), kind=kCustom, calls=%fused_computation.8 | custom fusion | bytes 24576 | tf_op jit(solution)/shard_map/gather | solution.py:115
  242.3 20.8 %gather_fusion.10 = f32[2048,3]{1,0:T(8,128)S(1)} fusion(f32[3,256,128]{0,2,1:T(8,128)} %copy.90, s32[2048]{0:T(1024)S(1)} %bitcast.100), kind=kCustom, calls=%fused_computation.10 | custom fusion | bytes 65536 | tf_op jit(solution)/shard_map/gather | solution.py:116
  263.5 80.3 %psum.14 = f32[3,2048]{0,1:T(8,128)S(1)} all-reduce(f32[3,2048]{0,1:T(8,128)S(1)} %select_bitcast_fusion), channel_id=1, replica_groups=mesh['row'=8,'col'=16] {'row','col'}, use_global_device_ids=true, to_apply=%region_4.5 | all-reduce | flops 6144 | bytes 49152 | tf_op jit(solution)/shard_map/psum | solution.py:118
  344.3 586.7 %while.16 = (s32[]{:T(128)}, f32[256,6]{0,1:T(8,128)S(1)}, f32[256]{0:T(256)S(1)}, f32[6,2048,128]{2,1,0:T(8,128)}, f32[3,256]{1,0:T(4,128)S(1)}, /*index=5*/s32...) while((s32[]{:T(128)}, f32[256,6]{0,1:T(8,128)S(1)}, ...), condition=%wide.region_8.9_spmd.clone, body=%wide.region_6.8_spmd.clone.sunk | while | flops 478678016 | bytes 36061472 | solution.py:69
  346.8 25.7 %sqrt_multiply_fusion.2 = f32[256,16384]{0,1:T(8,128)S(1)} fusion(f32[3,256]{1,0:T(4,128)S(1)} %get-tuple-element.277, f32[16384]{0:T(1024)S(1)} %bitcast.107, f32[256]{0:T(256)S(1)} %get-tuple-element.275, f32[1,3,128,128]{3,2,1,0:T(8,128)S(1)} %get-tuple-element.240), kind=kOutput, calls=%fused_computation.15.clone.1 | convolution fusion | flops 171966464 | bytes 17043456 | tf_op jit(solution)/shard_map/while/body/eval_jaxpr/dot_general | solution.py:38
  372.4 8.8 fusion.67
  383.4 25.7 %sqrt_multiply_fusion.2 = f32[256,16384]{0,1:T(8,128)S(1)} fusion(f32[3,256]{1,0:T(4,128)S(1)} %get-tuple-element.277, f32[16384]{0:T(1024)S(1)} %bitcast.107, f32[256]{0:T(256)S(1)} %get-tuple-element.275, f32[1,3,128,128]{3,2,1,0:T(8,128)S(1)} %get-tuple-element.240), kind=kOutput, calls=%fused_computation.15.clone.1 | convolution fusion | flops 171966464 | bytes 17043456 | tf_op jit(solution)/shard_map/while/body/eval_jaxpr/dot_general | solution.py:38
  409.1 8.8 fusion.67
  420.1 25.7 %sqrt_multiply_fusion.2 = f32[256,16384]{0,1:T(8,128)S(1)} fusion(f32[3,256]{1,0:T(4,128)S(1)} %get-tuple-element.277, f32[16384]{0:T(1024)S(1)} %bitcast.107, f32[256]{0:T(256)S(1)} %get-tuple-element.275, f32[1,3,128,128]{3,2,1,0:T(8,128)S(1)} %get-tuple-element.240), kind=kOutput, calls=%fused_computation.15.clone.1 | convolution fusion | flops 171966464 | bytes 17043456 | tf_op jit(solution)/shard_map/while/body/eval_jaxpr/dot_general | solution.py:38
  445.8 8.8 fusion.67
  456.8 25.7 %sqrt_multiply_fusion.2 = f32[256,16384]{0,1:T(8,128)S(1)} fusion(f32[3,256]{1,0:T(4,128)S(1)} %get-tuple-element.277, f32[16384]{0:T(1024)S(1)} %bitcast.107, f32[256]{0:T(256)S(1)} %get-tuple-element.275, f32[1,3,128,128]{3,2,1,0:T(8,128)S(1)} %get-tuple-element.240), kind=kOutput, calls=%fused_computation.15.clone.1 | convolution fusion | flops 171966464 | bytes 17043456 | tf_op jit(solution)/shard_map/while/body/eval_jaxpr/dot_general | solution.py:38
  482.4 8.8 fusion.67
  493.4 25.7 %sqrt_multiply_fusion.2 = f32[256,16384]{0,1:T(8,128)S(1)} fusion(f32[3,256]{1,0:T(4,128)S(1)} %get-tuple-element.277, f32[16384]{0:T(1024)S(1)} %bitcast.107, f32[256]{0:T(256)S(1)} %get-tuple-element.275, f32[1,3,128,128]{3,2,1,0:T(8,128)S(1)} %get-tuple-element.240), kind=kOutput, calls=%fused_computation.15.clone.1 | convolution fusion | flops 171966464 | bytes 17043456 | tf_op jit(solution)/shard_map/while/body/eval_jaxpr/dot_general | solution.py:38
  519.1 8.8 fusion.67
  530.1 25.7 %sqrt_multiply_fusion.2 = f32[256,16384]{0,1:T(8,128)S(1)} fusion(f32[3,256]{1,0:T(4,128)S(1)} %get-tuple-element.277, f32[16384]{0:T(1024)S(1)} %bitcast.107, f32[256]{0:T(256)S(1)} %get-tuple-element.275, f32[1,3,128,128]{3,2,1,0:T(8,128)S(1)} %get-tuple-element.240), kind=kOutput, calls=%fused_computation.15.clone.1 | convolution fusion | flops 171966464 | bytes 17043456 | tf_op jit(solution)/shard_map/while/body/eval_jaxpr/dot_general | solution.py:38
  555.7 8.8 fusion.67
  566.7 25.7 %sqrt_multiply_fusion.2 = f32[256,16384]{0,1:T(8,128)S(1)} fusion(f32[3,256]{1,0:T(4,128)S(1)} %get-tuple-element.277, f32[16384]{0:T(1024)S(1)} %bitcast.107, f32[256]{0:T(256)S(1)} %get-tuple-element.275, f32[1,3,128,128]{3,2,1,0:T(8,128)S(1)} %get-tuple-element.240), kind=kOutput, calls=%fused_computation.15.clone.1 | convolution fusion | flops 171966464 | bytes 17043456 | tf_op jit(solution)/shard_map/while/body/eval_jaxpr/dot_general | solution.py:38
  603.4 25.7 %sqrt_multiply_fusion.2 = f32[256,16384]{0,1:T(8,128)S(1)} fusion(f32[3,256]{1,0:T(4,128)S(1)} %get-tuple-element.277, f32[16384]{0:T(1024)S(1)} %bitcast.107, f32[256]{0:T(256)S(1)} %get-tuple-element.275, f32[1,3,128,128]{3,2,1,0:T(8,128)S(1)} %get-tuple-element.240), kind=kOutput, calls=%fused_computation.15.clone.1 | convolution fusion | flops 171966464 | bytes 17043456 | tf_op jit(solution)/shard_map/while/body/eval_jaxpr/dot_general | solution.py:38
  640.0 25.7 %sqrt_multiply_fusion.2 = f32[256,16384]{0,1:T(8,128)S(1)} fusion(f32[3,256]{1,0:T(4,128)S(1)} %get-tuple-element.277, f32[16384]{0:T(1024)S(1)} %bitcast.107, f32[256]{0:T(256)S(1)} %get-tuple-element.275, f32[1,3,128,128]{3,2,1,0:T(8,128)S(1)} %get-tuple-element.240), kind=kOutput, calls=%fused_computation.15.clone.1 | convolution fusion | flops 171966464 | bytes 17043456 | tf_op jit(solution)/shard_map/while/body/eval_jaxpr/dot_general | solution.py:38
  676.7 25.7 %sqrt_multiply_fusion.2 = f32[256,16384]{0,1:T(8,128)S(1)} fusion(f32[3,256]{1,0:T(4,128)S(1)} %get-tuple-element.277, f32[16384]{0:T(1024)S(1)} %bitcast.107, f32[256]{0:T(256)S(1)} %get-tuple-element.275, f32[1,3,128,128]{3,2,1,0:T(8,128)S(1)} %get-tuple-element.240), kind=kOutput, calls=%fused_computation.15.clone.1 | convolution fusion | flops 171966464 | bytes 17043456 | tf_op jit(solution)/shard_map/while/body/eval_jaxpr/dot_general | solution.py:38
  713.4 25.7 %sqrt_multiply_fusion.2 = f32[256,16384]{0,1:T(8,128)S(1)} fusion(f32[3,256]{1,0:T(4,128)S(1)} %get-tuple-element.277, f32[16384]{0:T(1024)S(1)} %bitcast.107, f32[256]{0:T(256)S(1)} %get-tuple-element.275, f32[1,3,128,128]{3,2,1,0:T(8,128)S(1)} %get-tuple-element.240), kind=kOutput, calls=%fused_computation.15.clone.1 | convolution fusion | flops 171966464 | bytes 17043456 | tf_op jit(solution)/shard_map/while/body/eval_jaxpr/dot_general | solution.py:38
  750.0 25.7 %sqrt_multiply_fusion.2 = f32[256,16384]{0,1:T(8,128)S(1)} fusion(f32[3,256]{1,0:T(4,128)S(1)} %get-tuple-element.277, f32[16384]{0:T(1024)S(1)} %bitcast.107, f32[256]{0:T(256)S(1)} %get-tuple-element.275, f32[1,3,128,128]{3,2,1,0:T(8,128)S(1)} %get-tuple-element.240), kind=kOutput, calls=%fused_computation.15.clone.1 | convolution fusion | flops 171966464 | bytes 17043456 | tf_op jit(solution)/shard_map/while/body/eval_jaxpr/dot_general | solution.py:38
  786.7 25.7 %sqrt_multiply_fusion.2 = f32[256,16384]{0,1:T(8,128)S(1)} fusion(f32[3,256]{1,0:T(4,128)S(1)} %get-tuple-element.277, f32[16384]{0:T(1024)S(1)} %bitcast.107, f32[256]{0:T(256)S(1)} %get-tuple-element.275, f32[1,3,128,128]{3,2,1,0:T(8,128)S(1)} %get-tuple-element.240), kind=kOutput, calls=%fused_computation.15.clone.1 | convolution fusion | flops 171966464 | bytes 17043456 | tf_op jit(solution)/shard_map/while/body/eval_jaxpr/dot_general | solution.py:38
  823.3 25.7 %sqrt_multiply_fusion.2 = f32[256,16384]{0,1:T(8,128)S(1)} fusion(f32[3,256]{1,0:T(4,128)S(1)} %get-tuple-element.277, f32[16384]{0:T(1024)S(1)} %bitcast.107, f32[256]{0:T(256)S(1)} %get-tuple-element.275, f32[1,3,128,128]{3,2,1,0:T(8,128)S(1)} %get-tuple-element.240), kind=kOutput, calls=%fused_computation.15.clone.1 | convolution fusion | flops 171966464 | bytes 17043456 | tf_op jit(solution)/shard_map/while/body/eval_jaxpr/dot_general | solution.py:38
  860.0 25.7 %sqrt_multiply_fusion.2 = f32[256,16384]{0,1:T(8,128)S(1)} fusion(f32[3,256]{1,0:T(4,128)S(1)} %get-tuple-element.277, f32[16384]{0:T(1024)S(1)} %bitcast.107, f32[256]{0:T(256)S(1)} %get-tuple-element.275, f32[1,3,128,128]{3,2,1,0:T(8,128)S(1)} %get-tuple-element.240), kind=kOutput, calls=%fused_computation.15.clone.1 | convolution fusion | flops 171966464 | bytes 17043456 | tf_op jit(solution)/shard_map/while/body/eval_jaxpr/dot_general | solution.py:38
  896.7 25.7 %sqrt_multiply_fusion.2 = f32[256,16384]{0,1:T(8,128)S(1)} fusion(f32[3,256]{1,0:T(4,128)S(1)} %get-tuple-element.277, f32[16384]{0:T(1024)S(1)} %bitcast.107, f32[256]{0:T(256)S(1)} %get-tuple-element.275, f32[1,3,128,128]{3,2,1,0:T(8,128)S(1)} %get-tuple-element.240), kind=kOutput, calls=%fused_computation.15.clone.1 | convolution fusion | flops 171966464 | bytes 17043456 | tf_op jit(solution)/shard_map/while/body/eval_jaxpr/dot_general | solution.py:38
  931.7 37.0 %psum.15 = f32[3,256]{1,0:T(4,128)S(1)} all-reduce(f32[3,256]{1,0:T(4,128)S(1)} %fusion.41), channel_id=1, replica_groups=mesh['row'=8,'col'=16] {'col'}, use_global_device_ids=true, to_apply=%region_9.10 | all-reduce | flops 768 | bytes 6144 | tf_op jit(solution)/shard_map/psum | solution.py:127
  (129 shorter events, 192.1 us)
Async XLA Ops:
  27.9 140.4 %all-to-all-start = ((f32[3,256,128]{2,0,1:T(4,128)}), f32[3,256,128]{2,0,1:T(4,128)S(1)}, u32[]{:S(2)}, u32[]{:S(2)}) async-start(f32[3,256,128]{2,0,1:T(4,128)} %scatter_fusion), calls=%async_computation | async-start | bytes 1048576 | tf_op jit(solution)/shard_map/all_to_all | solution.py:95
  39.1 305.2 %all-gather.2.cloned.1.call-start = ((), (), s32[]{:S(2)}) async-start(), calls=%async_computation.1 | async-start | bytes 7077888 | tf_op jit(solution)/shard_map/all_gather | solution.py:125
  194.3 23.4 %copy-start = (s32[8,256]{1,0:T(8,128)S(1)}, s32[8,256]{1,0:T(8,128)}, u32[]{:S(2)}) copy-start(s32[8,256]{1,0:T(8,128)} %param.7) | copy-start | bytes 24580
Sparse Core Ops, SparseCore 0:
  217.9 75.4 all-gather.1
where the time goes:
time: 982 us; the launch traced here: 976 us
  matrix products  550 us (56%)
  local copies, waits for them, and re-layouts  239 us (24%)
  blocking collectives  117 us (12%)
  other arithmetic  42.8 us (4%)
  between operations  14.6 us (1%)
  starting transfers between devices  11.2 us (1%)
    dot_general x16, matrix products, panel_sums(): lax.dot_general(targets, centres, (((0,), (0,)), ((), ())), precision=lax...  410 us
    dot_general x16, matrix products, panel_sums(): lax.dot_general(weights, features, (((1,), (1,)), ((), ())), precision=la...  140 us
    psum x1, blocking collectives, shards(): all_targets = lax.psum(local_targets, ('row', 'col'))  80.3 us
    scatter x1, local copies, waits for them, and re-layouts, shards(): precedes = jnp.zeros_like(follows).at[follows].set(counter)  60.5 us
    scatter x1, local copies, waits for them, and re-layouts, shards(): held_ids = jnp.full((held_slots,), blocks_all, jnp.int32).at[jnp.where(is...  60.3 us
    psum x1, blocking collectives, shards(): summed = lax.psum(partial_velocity, 'col')  37 us
    gather x2, local copies, waits for them, and re-layouts, shards(): picked = smoothed[:, places[wanted_block], wanted_point]  32.6 us
  transfers between devices with their start and end apart: 2, of which 0 were waited for; matrix products, arithmetic and copies ran while one was open for 18% of the time, Pallas kernels for 0%

commit v1 on v0

--- a/solution.py
+++ b/solution.py
@@ -115,7 +115,7 @@
     wanted_mine = owners[wanted_block] == my_index
     picked = smoothed[:, places[wanted_block], wanted_point]
     local_targets = jnp.where(wanted_mine[None, :], picked, 0.0)
-    all_targets = lax.psum(local_targets, ("row", "col"))
+    all_targets = lax.psum(lax.psum(local_targets, "row"), "col")
     panel = panel_points.shape[1]
     col_count = lax.axis_size("col")
     share = panel // col_count

time: 982 us -> 1050 us (1.069)
  blocking collectives: 117 us -> 183 us
    psum x1 -> x2, blocking collectives: 80.3 us -> 150 us  [shards(): all_targets = lax.psum(lax.psum(local_targets, 'row'), 'col')]
  transfers between devices with their start and end apart: 2 -> 2, of which waited for: 0 -> 0; matrix products, arithmetic and copies ran while one was open for 18% -> 17% of each run, Pallas kernels for 0% -> 0%
where the time goes in v1:
time: 1050 us; the launch traced here: 1040 us
  matrix products  551 us (52%)
  local copies, waits for them, and re-layouts  239 us (23%)
  blocking collectives  183 us (17%)
  other arithmetic  42.8 us (4%)
  between operations  14.6 us (1%)
  starting transfers between devices  11.2 us (1%)
    dot_general x16, matrix products, panel_sums(): lax.dot_general(targets, centres, (((0,), (0,)), ((), ())), precision=lax...  411 us
    psum x2, blocking collectives, shards(): all_targets = lax.psum(lax.psum(local_targets, 'row'), 'col')  150 us
    dot_general x16, matrix products, panel_sums(): lax.dot_general(weights, features, (((1,), (1,)), ((), ())), precision=la...  140 us
    scatter x1, local copies, waits for them, and re-layouts, shards(): precedes = jnp.zeros_like(follows).at[follows].set(counter)  60.5 us
    scatter x1, local copies, waits for them, and re-layouts, shards(): held_ids = jnp.full((held_slots,), blocks_all, jnp.int32).at[jnp.where(is...  60.3 us
    psum x1, blocking collectives, shards(): summed = lax.psum(partial_velocity, 'col')  33.2 us
    gather x2, local copies, waits for them, and re-layouts, shards(): picked = smoothed[:, places[wanted_block], wanted_point]  32.6 us
  transfers between devices with their start and end apart: 2, of which 0 were waited for; matrix products, arithmetic and copies ran while one was open for 17% of the time, Pallas kernels for 0%

profile of v1, /device:TPU:0, one launch (start us, length us, event | category | flops | bytes accessed | tf_op | source)
XLA Modules:
  0.0 1042.0 jit_solution(1483917200932947082)
XLA Ops:
  15.4 12.5 %scatter_fusion = f32[3,256,128]{2,0,1:T(4,128)} fusion(f32[3,256,128]{2,0,1:T(4,128)} %broadcast_in_dim.36, s32[128]{0:T(128)S(1)} %compare_select_fusion.13, f32[128,3,128]{2,1,0:T(4,128)S(1)} %copy.77), kind=kCustom, calls=%fused_computation.12 | custom fusion | bytes 590336 | tf_op jit(solution)/shard_map/scatter | solution.py:93
  27.9 11.2 %all-to-all-start = ((f32[3,256,128]{2,0,1:T(4,128)}), f32[3,256,128]{2,0,1:T(4,128)S(1)}, u32[]{:S(2)}, u32[]{:S(2)}) async-start(f32[3,256,128]{2,0,1:T(4,128)} %scatter_fusion), calls=%async_computation | async-start | bytes 1048576 | tf_op jit(solution)/shard_map/all_to_all | solution.py:95
  40.4 60.3 %scatter_custom_fusion.1 = s32[256]{0:T(256)S(1)} fusion(s32[16384]{0:T(1024)S(1)} %bitcast.119, s32[16384]{0:T(1024)S(1)} %iota.31, s32[]{:T(128)} %constant.150.clone.1), kind=kCustom, calls=%fused_computation.120 | custom fusion | bytes 1028 | tf_op jit(solution)/shard_map/scatter | solution.py:100
  100.8 60.5 %scatter_custom_fusion.2 = s32[16384]{0:T(1024)S(1)} fusion(s32[16384]{0:T(1024)S(1)} %bitcast.118, s32[16384]{0:T(1024)S(1)} %iota.33, s32[]{:T(128)} %constant.144.clone.1), kind=kCustom, calls=%fused_computation.79 | custom fusion | bytes 65540 | tf_op jit(solution)/shard_map/scatter | solution.py:83
  217.9 11.8 %gather_fusion.9 = s32[2048]{0:T(1024)S(1)} fusion(s32[16384]{0:T(1024)S(1)} %fusion.28, s32[2048]{0:T(1024)S(1)} %broadcast_clamp_fusion), kind=kCustom, calls=%fused_computation.9 | custom fusion | bytes 24576 | tf_op jit(solution)/shard_map/gather | solution.py:116
  229.7 11.8 %gather_fusion.8 = s32[2048]{0:T(1024)S(1)} fusion(s32[16384]{0:T(1024)S(1)} %bitcast.99, s32[2048]{0:T(1024)S(1)} %broadcast_clamp_fusion), kind=kCustom, calls=%fused_computation.8 | custom fusion | bytes 24576 | tf_op jit(solution)/shard_map/gather | solution.py:115
  242.3 20.8 %gather_fusion.10 = f32[2048,3]{1,0:T(8,128)S(1)} fusion(f32[3,256,128]{0,2,1:T(8,128)} %copy.90, s32[2048]{0:T(1024)S(1)} %bitcast.100), kind=kCustom, calls=%fused_computation.10 | custom fusion | bytes 65536 | tf_op jit(solution)/shard_map/gather | solution.py:116
  263.5 73.2 %psum.21 = f32[3,2048]{0,1:T(8,128)S(1)} all-reduce(f32[3,2048]{0,1:T(8,128)S(1)} %select_bitcast_fusion), channel_id=1, replica_groups=mesh['row'=8,'col'=16] {'row'}, use_global_device_ids=true, to_apply=%region_4.5 | all-reduce | flops 6144 | bytes 49152 | tf_op jit(solution)/shard_map/psum | solution.py:118
  336.6 76.5 %psum.22 = f32[3,2048]{0,1:T(8,128)S(1)} all-reduce(f32[3,2048]{0,1:T(8,128)S(1)} %psum.21), channel_id=1, replica_groups=mesh['row'=8,'col'=16] {'col'}, use_global_device_ids=true, to_apply=%region_5.6 | all-reduce | flops 6144 | bytes 49152 | tf_op jit(solution)/shard_map/psum | solution.py:118
  413.7 586.9 %while.16 = (s32[]{:T(128)}, f32[256,6]{0,1:T(8,128)S(1)}, f32[256]{0:T(256)S(1)}, f32[6,2048,128]{2,1,0:T(8,128)}, f32[3,256]{1,0:T(4,128)S(1)}, /*index=5*/s32...) while((s32[]{:T(128)}, f32[256,6]{0,1:T(8,128)S(1)}, ...), condition=%wide.region_9.10_spmd.clone, body=%wide.region_7.9_spmd.clone.sunk | while | flops 478678016 | bytes 36061472 | solution.py:69
  416.1 25.7 %sqrt_multiply_fusion.2 = f32[256,16384]{0,1:T(8,128)S(1)} fusion(f32[3,256]{1,0:T(4,128)S(1)} %get-tuple-element.277, f32[16384]{0:T(1024)S(1)} %bitcast.107, f32[256]{0:T(256)S(1)} %get-tuple-element.275, f32[1,3,128,128]{3,2,1,0:T(8,128)S(1)} %get-tuple-element.240), kind=kOutput, calls=%fused_computation.15.clone.1 | convolution fusion | flops 171966464 | bytes 17043456 | tf_op jit(solution)/shard_map/while/body/eval_jaxpr/dot_general | solution.py:38
  441.8 8.8 fusion.67
  452.8 25.7 %sqrt_multiply_fusion.2 = f32[256,16384]{0,1:T(8,128)S(1)} fusion(f32[3,256]{1,0:T(4,128)S(1)} %get-tuple-element.277, f32[16384]{0:T(1024)S(1)} %bitcast.107, f32[256]{0:T(256)S(1)} %get-tuple-element.275, f32[1,3,128,128]{3,2,1,0:T(8,128)S(1)} %get-tuple-element.240), kind=kOutput, calls=%fused_computation.15.clone.1 | convolution fusion | flops 171966464 | bytes 17043456 | tf_op jit(solution)/shard_map/while/body/eval_jaxpr/dot_general | solution.py:38
  478.5 8.8 fusion.67
  489.5 25.7 %sqrt_multiply_fusion.2 = f32[256,16384]{0,1:T(8,128)S(1)} fusion(f32[3,256]{1,0:T(4,128)S(1)} %get-tuple-element.277, f32[16384]{0:T(1024)S(1)} %bitcast.107, f32[256]{0:T(256)S(1)} %get-tuple-element.275, f32[1,3,128,128]{3,2,1,0:T(8,128)S(1)} %get-tuple-element.240), kind=kOutput, calls=%fused_computation.15.clone.1 | convolution fusion | flops 171966464 | bytes 17043456 | tf_op jit(solution)/shard_map/while/body/eval_jaxpr/dot_general | solution.py:38
  515.2 8.8 fusion.67
  526.2 25.7 %sqrt_multiply_fusion.2 = f32[256,16384]{0,1:T(8,128)S(1)} fusion(f32[3,256]{1,0:T(4,128)S(1)} %get-tuple-element.277, f32[16384]{0:T(1024)S(1)} %bitcast.107, f32[256]{0:T(256)S(1)} %get-tuple-element.275, f32[1,3,128,128]{3,2,1,0:T(8,128)S(1)} %get-tuple-element.240), kind=kOutput, calls=%fused_computation.15.clone.1 | convolution fusion | flops 171966464 | bytes 17043456 | tf_op jit(solution)/shard_map/while/body/eval_jaxpr/dot_general | solution.py:38
  551.8 8.8 fusion.67
  562.8 25.7 %sqrt_multiply_fusion.2 = f32[256,16384]{0,1:T(8,128)S(1)} fusion(f32[3,256]{1,0:T(4,128)S(1)} %get-tuple-element.277, f32[16384]{0:T(1024)S(1)} %bitcast.107, f32[256]{0:T(256)S(1)} %get-tuple-element.275, f32[1,3,128,128]{3,2,1,0:T(8,128)S(1)} %get-tuple-element.240), kind=kOutput, calls=%fused_computation.15.clone.1 | convolution fusion | flops 171966464 | bytes 17043456 | tf_op jit(solution)/shard_map/while/body/eval_jaxpr/dot_general | solution.py:38
  588.5 8.8 fusion.67
  599.5 25.7 %sqrt_multiply_fusion.2 = f32[256,16384]{0,1:T(8,128)S(1)} fusion(f32[3,256]{1,0:T(4,128)S(1)} %get-tuple-element.277, f32[16384]{0:T(1024)S(1)} %bitcast.107, f32[256]{0:T(256)S(1)} %get-tuple-element.275, f32[1,3,128,128]{3,2,1,0:T(8,128)S(1)} %get-tuple-element.240), kind=kOutput, calls=%fused_computation.15.clone.1 | convolution fusion | flops 171966464 | bytes 17043456 | tf_op jit(solution)/shard_map/while/body/eval_jaxpr/dot_general | solution.py:38
  636.2 25.7 %sqrt_multiply_fusion.2 = f32[256,16384]{0,1:T(8,128)S(1)} fusion(f32[3,256]{1,0:T(4,128)S(1)} %get-tuple-element.277, f32[16384]{0:T(1024)S(1)} %bitcast.107, f32[256]{0:T(256)S(1)} %get-tuple-element.275, f32[1,3,128,128]{3,2,1,0:T(8,128)S(1)} %get-tuple-element.240), kind=kOutput, calls=%fused_computation.15.clone.1 | convolution fusion | flops 171966464 | bytes 17043456 | tf_op jit(solution)/shard_map/while/body/eval_jaxpr/dot_general | solution.py:38
  672.8 25.7 %sqrt_multiply_fusion.2 = f32[256,16384]{0,1:T(8,128)S(1)} fusion(f32[3,256]{1,0:T(4,128)S(1)} %get-tuple-element.277, f32[16384]{0:T(1024)S(1)} %bitcast.107, f32[256]{0:T(256)S(1)} %get-tuple-element.275, f32[1,3,128,128]{3,2,1,0:T(8,128)S(1)} %get-tuple-element.240), kind=kOutput, calls=%fused_computation.15.clone.1 | convolution fusion | flops 171966464 | bytes 17043456 | tf_op jit(solution)/shard_map/while/body/eval_jaxpr/dot_general | solution.py:38
  709.5 25.7 %sqrt_multiply_fusion.2 = f32[256,16384]{0,1:T(8,128)S(1)} fusion(f32[3,256]{1,0:T(4,128)S(1)} %get-tuple-element.277, f32[16384]{0:T(1024)S(1)} %bitcast.107, f32[256]{0:T(256)S(1)} %get-tuple-element.275, f32[1,3,128,128]{3,2,1,0:T(8,128)S(1)} %get-tuple-element.240), kind=kOutput, calls=%fused_computation.15.clone.1 | convolution fusion | flops 171966464 | bytes 17043456 | tf_op jit(solution)/shard_map/while/body/eval_jaxpr/dot_general | solution.py:38
  746.2 25.7 %sqrt_multiply_fusion.2 = f32[256,16384]{0,1:T(8,128)S(1)} fusion(f32[3,256]{1,0:T(4,128)S(1)} %get-tuple-element.277, f32[16384]{0:T(1024)S(1)} %bitcast.107, f32[256]{0:T(256)S(1)} %get-tuple-element.275, f32[1,3,128,128]{3,2,1,0:T(8,128)S(1)} %get-tuple-element.240), kind=kOutput, calls=%fused_computation.15.clone.1 | convolution fusion | flops 171966464 | bytes 17043456 | tf_op jit(solution)/shard_map/while/body/eval_jaxpr/dot_general | solution.py:38
  782.8 25.7 %sqrt_multiply_fusion.2 = f32[256,16384]{0,1:T(8,128)S(1)} fusion(f32[3,256]{1,0:T(4,128)S(1)} %get-tuple-element.277, f32[16384]{0:T(1024)S(1)} %bitcast.107, f32[256]{0:T(256)S(1)} %get-tuple-element.275, f32[1,3,128,128]{3,2,1,0:T(8,128)S(1)} %get-tuple-element.240), kind=kOutput, calls=%fused_computation.15.clone.1 | convolution fusion | flops 171966464 | bytes 17043456 | tf_op jit(solution)/shard_map/while/body/eval_jaxpr/dot_general | solution.py:38
  819.5 25.7 %sqrt_multiply_fusion.2 = f32[256,16384]{0,1:T(8,128)S(1)} fusion(f32[3,256]{1,0:T(4,128)S(1)} %get-tuple-element.277, f32[16384]{0:T(1024)S(1)} %bitcast.107, f32[256]{0:T(256)S(1)} %get-tuple-element.275, f32[1,3,128,128]{3,2,1,0:T(8,128)S(1)} %get-tuple-element.240), kind=kOutput, calls=%fused_computation.15.clone.1 | convolution fusion | flops 171966464 | bytes 17043456 | tf_op jit(solution)/shard_map/while/body/eval_jaxpr/dot_general | solution.py:38
  856.2 25.7 %sqrt_multiply_fusion.2 = f32[256,16384]{0,1:T(8,128)S(1)} fusion(f32[3,256]{1,0:T(4,128)S(1)} %get-tuple-element.277, f32[16384]{0:T(1024)S(1)} %bitcast.107, f32[256]{0:T(256)S(1)} %get-tuple-element.275, f32[1,3,128,128]{3,2,1,0:T(8,128)S(1)} %get-tuple-element.240), kind=kOutput, calls=%fused_computation.15.clone.1 | convolution fusion | flops 171966464 | bytes 17043456 | tf_op jit(solution)/shard_map/while/body/eval_jaxpr/dot_general | solution.py:38
  892.8 25.7 %sqrt_multiply_fusion.2 = f32[256,16384]{0,1:T(8,128)S(1)} fusion(f32[3,256]{1,0:T(4,128)S(1)} %get-tuple-element.277, f32[16384]{0:T(1024)S(1)} %bitcast.107, f32[256]{0:T(256)S(1)} %get-tuple-element.275, f32[1,3,128,128]{3,2,1,0:T(8,128)S(1)} %get-tuple-element.240), kind=kOutput, calls=%fused_computation.15.clone.1 | convolution fusion | flops 171966464 | bytes 17043456 | tf_op jit(solution)/shard_map/while/body/eval_jaxpr/dot_general | solution.py:38
  929.5 25.7 %sqrt_multiply_fusion.2 = f32[256,16384]{0,1:T(8,128)S(1)} fusion(f32[3,256]{1,0:T(4,128)S(1)} %get-tuple-element.277, f32[16384]{0:T(1024)S(1)} %bitcast.107, f32[256]{0:T(256)S(1)} %get-tuple-element.275, f32[1,3,128,128]{3,2,1,0:T(8,128)S(1)} %get-tuple-element.240), kind=kOutput, calls=%fused_computation.15.clone.1 | convolution fusion | flops 171966464 | bytes 17043456 | tf_op jit(solution)/shard_map/while/body/eval_jaxpr/dot_general | solution.py:38
  966.2 25.7 %sqrt_multiply_fusion.2 = f32[256,16384]{0,1:T(8,128)S(1)} fusion(f32[3,256]{1,0:T(4,128)S(1)} %get-tuple-element.277, f32[16384]{0:T(1024)S(1)} %bitcast.107, f32[256]{0:T(256)S(1)} %get-tuple-element.275, f32[1,3,128,128]{3,2,1,0:T(8,128)S(1)} %get-tuple-element.240), kind=kOutput, calls=%fused_computation.15.clone.1 | convolution fusion | flops 171966464 | bytes 17043456 | tf_op jit(solution)/shard_map/while/body/eval_jaxpr/dot_general | solution.py:38
  1001.2 33.2 %psum.23 = f32[3,256]{1,0:T(4,128)S(1)} all-reduce(f32[3,256]{1,0:T(4,128)S(1)} %fusion.41), channel_id=1, replica_groups=mesh['row'=8,'col'=16] {'col'}, use_global_device_ids=true, to_apply=%region_10.11 | all-reduce | flops 768 | bytes 6144 | tf_op jit(solution)/shard_map/psum | solution.py:127
  (130 shorter events, 200.9 us)
Async XLA Ops:
  27.9 140.4 %all-to-all-start = ((f32[3,256,128]{2,0,1:T(4,128)}), f32[3,256,128]{2,0,1:T(4,128)S(1)}, u32[]{:S(2)}, u32[]{:S(2)}) async-start(f32[3,256,128]{2,0,1:T(4,128)} %scatter_fusion), calls=%async_computation | async-start | bytes 1048576 | tf_op jit(solution)/shard_map/all_to_all | solution.py:95
  39.1 374.6 %all-gather.2.cloned.1.call-start = ((), (), s32[]{:S(2)}) async-start(), calls=%async_computation.1 | async-start | bytes 7077888 | tf_op jit(solution)/shard_map/all_gather | solution.py:125
  194.3 23.4 %copy-start = (s32[8,256]{1,0:T(8,128)S(1)}, s32[8,256]{1,0:T(8,128)}, u32[]{:S(2)}) copy-start(s32[8,256]{1,0:T(8,128)} %param.7) | copy-start | bytes 24580
Sparse Core Ops, SparseCore 0:
  217.9 80.3 all-gather.1
